TPU v7x, 32 devices: a whole 2x2x4 slice. The times are simulated.
32 devices in a mesh: copies: 2 (over x), expert: 4 (over y, core), tm: 4 (over z).
Axes of the slice: x: 2, y: 2, z: 4, core: 2. Of those that a mesh axis runs over, the one named last changes fastest.
Arguments:
- tokens: bfloat16 [4, 1024, 2048], P('tm', ('copies', 'expert')), parts along dimension 1, may hold values from -6 to 6
- route_ids: int32 [4, 1024, 6], P('tm', ('copies', 'expert')), parts along dimension 1, may hold values from 0 to 15, all different within a row; in each aligned block of 128 rows (0 to 127, 128 to 255, ..., all dimensions but the last counted through in order) at most 72 rows name the same one
- route_probs: float32 [4, 1024, 6], P('tm', ('copies', 'expert')), parts along dimension 1, may hold values from 0.05 to 1
- step_size: float32 [8], P(('copies', 'tm')), parts along dimension 0, may hold values from 0.2 to 0.6
- start_state: float32 [1024, 2048], P(('copies', 'expert')), parts along dimension 0, may hold values from -6 to 6
- w_gate: bfloat16 [16, 2048, 768], P('expert'), may hold values from -0.125 to 0.125
- w_up: bfloat16 [16, 2048, 768], P('expert'), may hold values from -0.125 to 0.125
- w_down: bfloat16 [16, 768, 2048], P('expert'), may hold values from -0.21875 to 0.21875
Outputs:
- new_iterate: float32 [4, 1024, 2048], P('tm', ('copies', 'expert')), parts along dimension 1
There are 2 independent parts, one for each index of `copies`. A program takes and returns all parts, laid end to end along the dimension named above; an argument that names none is the same for every part. Nothing has to cross between parts.
Inputs may be any that keep to these rules, and one draw needn't show every extreme that they name: `route_ids`: each row names 6 different experts. In each aligned block of 128 rows (the tokens of one device), no expert is named by more than 72 rows, a bound that some block reaches.
All inputs are finite; a program needn't handle non-finite values.
Results may differ from a plain program's by a relative error of at most 0.0018.
Values may be sent and summed in bfloat16 or wider, within the bound.
A program may use at most 128 MiB of HBM per device.

v0:
```python
import jax
import jax.numpy as jnp
from jax import lax
from jax.sharding import PartitionSpec as P


def expert_rows(received, w_gate, w_up, w_down):
    local_count, source_count, slot_count, feature_count = received.shape
    flat_rows = received.reshape(local_count, source_count * slot_count, feature_count)
    gate_act = jnp.einsum("jrd,jdf->jrf", flat_rows, w_gate, preferred_element_type=jnp.float32)
    up_act = jnp.einsum("jrd,jdf->jrf", flat_rows, w_up, preferred_element_type=jnp.float32)
    hidden = (jax.nn.silu(gate_act) * up_act).astype(jnp.bfloat16)
    result = jnp.einsum("jrf,jfd->jrd", hidden, w_down, preferred_element_type=jnp.float32)
    return result.astype(jnp.bfloat16).reshape(local_count, source_count, slot_count, feature_count)


def shards(tokens, route_ids, route_probs, step_size, start_state, w_gate, w_up, w_down):
    tok_count = tokens.shape[1]
    feature_count = tokens.shape[2]
    topk_count = route_ids.shape[2]
    expert_total = w_gate.shape[0] * lax.axis_size("expert")
    capacity = 3 * tok_count * topk_count // (2 * expert_total)
    values = tokens[0].astype(jnp.float32)
    normed = (values * lax.rsqrt(jnp.mean(values * values, axis=-1, keepdims=True) + 1e-06)).astype(
        jnp.bfloat16
    )
    flat_ids = route_ids[0].reshape(-1)
    one_hot = (flat_ids[:, None] == jnp.arange(expert_total, dtype=jnp.int32)[None, :]).astype(
        jnp.int32
    )
    earlier = jnp.cumsum(one_hot, axis=0) - one_hot
    position = jnp.sum(earlier * one_hot, axis=1)
    slot_index = flat_ids * capacity + position
    slot_grid = slot_index[:, None] == jnp.arange(expert_total * capacity, dtype=jnp.int32)[None, :]
    dispatch_map = jnp.any(slot_grid.reshape(tok_count, topk_count, -1), axis=1).astype(
        jnp.bfloat16
    )
    packed = jnp.einsum(
        "ts,td->sd", dispatch_map, normed, preferred_element_type=jnp.float32
    ).astype(jnp.bfloat16)
    outgoing = packed.reshape(expert_total, 1, capacity, feature_count)
    received = lax.all_to_all(outgoing, "expert", split_axis=0, concat_axis=1, tiled=True)
    answered = expert_rows(received, w_gate, w_up, w_down)
    returned = lax.all_to_all(answered, "expert", split_axis=1, concat_axis=0, tiled=True)
    gathered = returned.reshape(expert_total * capacity, feature_count)[slot_index]
    gathered = gathered.reshape(tok_count, topk_count, feature_count).astype(jnp.float32)
    gate_probs = route_probs[0]
    weights = gate_probs / jnp.sum(gate_probs, axis=-1, keepdims=True)
    drift_rows = jnp.einsum("tk,tkd->td", weights, gathered, precision=lax.Precision.HIGHEST)
    increment = step_size[0] * drift_rows
    own_index = lax.axis_index("tm")
    shard_rows = lax.all_gather(
        increment[None].astype(jnp.bfloat16), "tm", axis=0, tiled=True
    ).astype(jnp.float32)
    below_own = jnp.arange(shard_rows.shape[0], dtype=jnp.int32) <= own_index
    summed = jnp.zeros_like(increment) + jnp.sum(
        jnp.where(below_own[:, None, None], shard_rows, 0.0), axis=0
    )
    return (start_state + summed)[None]


def solution(mesh):
    return jax.shard_map(
        shards,
        mesh=mesh,
        in_specs=(
            P("tm", ("copies", "expert"), None),
            P("tm", ("copies", "expert"), None),
            P("tm", ("copies", "expert"), None),
            P(("copies", "tm")),
            P(("copies", "expert"), None),
            P("expert", None, None),
            P("expert", None, None),
            P("expert", None, None),
        ),
        out_specs=P("tm", ("copies", "expert"), None),
        check_vma=False,
    )
```

profile of v0, /device:TPU:24, one launch (start us, length us, event | category | flops | bytes accessed | tf_op | source)
XLA Modules:
  0.0 233.3 jit_solution(10654996169284588786)
XLA Ops:
  6.5 0.8 copy.25
  7.3 0.1 eq.43
  7.5 0.1 eq.39
  7.6 1.7 reduce-window.6
  9.3 0.3 slice_reduce_fusion
  9.6 0.1 fusion.11
  9.7 0.1 reduce_sum.42
  9.9 0.1 copy.29
  9.9 0.6 fusion.1
  10.5 1.2 fusion.3
  11.8 0.0 slice-start
  11.8 2.7 %convolution_convert_fusion = bf16[1152,2048]{1,0:T(8,128)(2,1)S(1)} fusion(pred[128,1152]{1,0:T(8,128)(4,1)S(1)} %fusion.1, bf16[1,128,2048]{2,1,0:T(8,128)(2,1)} %param.8, f32[128]{0:T(128)S(1)} %add_rsqrt_fusion), kind=kOutput, calls=%fused_computation.1 | convolution fusion | flops 607125504 | bytes 5390848 | tf_op jit(solution)/shard_map/ts,td->sd/dot_general | solution.py:38
  14.4 0.0 slice-start.1
  14.5 56.6 %all_to_all.30 = bf16[16,1,72,2048]{3,2,1,0:T(8,128)(2,1)S(1)} all-to-all(bf16[16,1,72,2048]{3,2,1,0:T(8,128)(2,1)S(1)} %bitcast.66), channel_id=1, replica_groups=mesh['copies'=2,'expert'=4,'tm'=4] {'expert'}, dimensions={0} | all-to-all | bytes 9437184 | tf_op jit(solution)/shard_map/all_to_all | solution.py:42
  71.1 0.0 slice-start.2
  71.1 0.7 copy.31
  71.8 0.0 copy-start
  71.8 2.2 copy-done
  74.0 0.0 slice-done
  74.0 0.0 slice-done.1
  74.0 0.6 slice-done.2
  74.6 5.7 %fusion.16 = f32[4,288,768]{2,1,0:T(8,128)} fusion(bf16[4,288,2048]{2,1,0:T(8,128)(2,1)S(1)} %bitcast.68, bf16[4,2048,768]{2,1,0:T(8,128)(2,1)S(1)} %bitcast.74), kind=kOutput, calls=%fused_computation.37 | convolution fusion | flops 3623878656 | bytes 20840448 | tf_op jit(solution)/shard_map/jrd,jdf->jrf/dot_general | solution.py:10
  80.2 15.9 %convolution_convert_fusion.1 = bf16[4,288,2048]{2,1,0:T(8,128)(2,1)} fusion(bf16[4,768,2048]{2,1,0:T(8,128)(2,1)} %param.15, f32[4,288,768]{2,1,0:T(8,128)} %fusion.16, bf16[4,288,2048]{2,1,0:T(8,128)(2,1)} %bitcast.69, bf16[4,2048,768]{2,1,0:T(8,128)(2,1)} %param.14), kind=kOutput, calls=%fused_computation.4 | convolution fusion | flops 7255425024 | bytes 38141952 | tf_op jit(solution)/shard_map/jrf,jfd->jrd/dot_general | solution.py:13
  96.1 5.2 %copy.32 = bf16[4,4,72,2048]{3,2,0,1:T(8,128)(2,1)} copy(bf16[4,4,72,2048]{3,2,1,0:T(8,128)(2,1)} %bitcast.70) | data formatting | bytes 9437184 | tf_op jit(solution)/shard_map/reshape | solution.py:14
  101.3 0.0 copy-start.2
  101.3 5.1 %all-to-all-start.1 = ((bf16[4,4,72,2048]{3,2,0,1:T(8,128)(2,1)}), bf16[4,4,72,2048]{3,2,0,1:T(8,128)(2,1)}, u32[]{:S(2)}, u32[]{:S(2)}) async-start(bf16[4,4,72,2048]{3,2,0,1:T(8,128)(2,1)} %copy.32), calls=%async_computation.1 | async-start | bytes 9437184 | tf_op jit(solution)/shard_map/all_to_all | solution.py:44
  106.4 0.2 all-gather.3.cloned.1.call-start
  106.6 0.1 mul.59
  106.8 0.0 copy-done.2
  106.8 0.1 copy.33
  107.6 52.6 %all-to-all-done.1 = bf16[4,4,72,2048]{3,2,0,1:T(8,128)(2,1)} async-done(((bf16[4,4,72,2048]{3,2,0,1:T(8,128)(2,1)}), bf16[4,4,72,2048]{3,2,0,1:T(8,128)(2,1)}, u32[]{:S(2)}, u32[]{:S(2)}) %all-to-all-start.1) | async-done | bytes 4718624 | tf_op jit(solution)/shard_map/all_to_all | solution.py:44
  160.2 9.3 %gather_fusion = bf16[768,2048]{1,0:T(8,128)(2,1)S(1)} fusion(bf16[1152,2048]{1,0:T(8,128)(2,1)} %bitcast.15, s32[1024]{0:T(1024)S(1)} %pad_clamp_fusion), kind=kCustom, calls=%fused_computation | custom fusion | bytes 6294528 | tf_op jit(solution)/shard_map/gather | solution.py:45
  169.5 2.9 %reshape.100 = bf16[128,6,2048]{2,1,0:T(8,128)(2,1)} reshape(bf16[768,2048]{1,0:T(8,128)(2,1)S(1)} %gather_fusion) | data formatting | bytes 6291456 | tf_op jit(solution)/shard_map/reshape | solution.py:46
  172.4 0.0 copy-start.1
  172.4 5.7 %fusion.17 = f32[128,1,2048]{2,1,0:T(1,128)S(1)} fusion(f32[128,6,1]{1,2,0:T(1,128)S(1)} %copy.33, bf16[128,6,2048]{2,1,0:T(8,128)(2,1)} %reshape.100), kind=kOutput, calls=%fused_computation.38 | convolution fusion | flops 18874368 | bytes 4197376 | tf_op jit(solution)/shard_map/tk,tkd->td/dot_general | solution.py:49
  178.1 1.1 fusion.5
  179.2 0.0 all-gather.3.cloned.1.call-update
  179.2 43.9 %all-gather.3.cloned.1.call-done = bf16[512,2048]{1,0:T(8,128)(2,1)} async-done(((bf16[128,2048]{1,0:T(8,128)(2,1)}), bf16[512,2048]{1,0:T(8,128)(2,1)}) %all-gather.3.cloned.1.call-update) | async-done | bytes 2097168 | tf_op jit(solution)/shard_map/all_gather | solution.py:52
  223.1 2.2 fusion
  225.3 0.0 copy-done.1
  225.4 1.1 add_bitcast_fusion
  (11 shorter events, 0.1 us)
Async XLA Ops:
  11.8 62.2 %slice-start = ((s8[12582912]{0:T(1024)(128)(4,1)}), s8[4194304]{0:T(1024)(128)(4,1)S(1)}, s32[]{:S(2)}) async-start(s8[12582912]{0:T(1024)(128)(4,1)} %bitcast.73), calls=%async_computation.3 | async-start | bytes 8388608
  14.4 59.6 %slice-start.1 = ((s8[12582912]{0:T(1024)(128)(4,1)}), s8[4194304]{0:T(1024)(128)(4,1)S(1)}, s32[]{:S(2)}) async-start(s8[12582912]{0:T(1024)(128)(4,1)} %bitcast.73), calls=%async_computation.4 | async-start | bytes 8388608
  71.1 3.5 %slice-start.2 = ((s8[12582912]{0:T(1024)(128)(4,1)}), s8[4194304]{0:T(1024)(128)(4,1)S(1)}, s32[]{:S(2)}) async-start(s8[12582912]{0:T(1024)(128)(4,1)} %bitcast.73), calls=%async_computation.5 | async-start | bytes 8388608
  71.8 2.2 copy-start
  101.3 5.5 %copy-start.2 = (f32[1,128,6]{1,0,2:T(1,128)S(1)}, f32[1,128,6]{1,0,2:T(1,128)}, u32[]{:S(2)}) copy-start(f32[1,128,6]{1,0,2:T(1,128)} %param.10) | copy-start | bytes 9220
  101.3 58.9 %all-to-all-start.1 = ((bf16[4,4,72,2048]{3,2,0,1:T(8,128)(2,1)}), bf16[4,4,72,2048]{3,2,0,1:T(8,128)(2,1)}, u32[]{:S(2)}, u32[]{:S(2)}) async-start(bf16[4,4,72,2048]{3,2,0,1:T(8,128)(2,1)} %copy.32), calls=%async_computation.1 | async-start | bytes 9437184 | tf_op jit(solution)/shard_map/all_to_all | solution.py:44
  106.4 116.7 %all-gather.3.cloned.1.call-start = ((), (), s32[]{:S(2)}) async-start(), calls=%async_computation.2 | async-start | bytes 2621440 | tf_op jit(solution)/shard_map/all_gather | solution.py:52
  172.4 53.0 %copy-start.1 = (f32[128,2048]{1,0:T(8,128)S(1)}, f32[128,2048]{1,0:T(8,128)}, u32[]{:S(2)}) copy-start(f32[128,2048]{1,0:T(8,128)} %param.12) | copy-start | bytes 3145732
Sparse Core Ops, SparseCore 0:
  179.3 43.7 all-gather.2
where the time goes:
time: 237 us; the launch traced here: 233 us
  waiting for transfers between devices  96.5 us (41%)
  blocking collectives  56.6 us (24%)
  matrix products  29.9 us (13%)
  local copies, waits for them, and re-layouts  22.6 us (10%)
  between operations  14.2 us (6%)
  other arithmetic  8.19 us (3%)
  starting transfers between devices  5.28 us (2%)
    all_to_all x1, blocking collectives, shards(): lax.all_to_all(outgoing, 'expert', split_axis=0, concat_axis=1, tiled=True)  56.6 us
    all_to_all x1, waiting for transfers between devices, shards(): lax.all_to_all(answered, 'expert', split_axis=1, concat_axis=0, tiled=True)  52.6 us
    all_gather x1, waiting for transfers between devices, shards(): lax.all_gather(increment[None].astype(jnp.bfloat16), 'tm', axis=0, tiled=...  43.9 us
    dot_general x1, matrix products, expert_rows(): jnp.einsum('jrf,jfd->jrd', hidden, w_down, preferred_element_type=jnp.flo...  15.9 us
    gather x1, local copies, waits for them, and re-layouts, shards(): returned.reshape(expert_total * capacity, feature_count)[slot_index]  9.28 us
    dot_general x1, matrix products, shards(): jnp.einsum('tk,tkd->td', weights, gathered, precision=lax.Precision.HIGHEST)  5.74 us
    dot_general x1, matrix products, expert_rows(): jnp.einsum('jrd,jdf->jrf', flat_rows, w_gate, preferred_element_type=jnp....  5.66 us
    reshape x1, local copies, waits for them, and re-layouts, expert_rows(): result.astype(jnp.bfloat16)  5.23 us
  transfers between devices with their start and end apart: 2, of which 2 were waited for; matrix products, arithmetic and copies ran while one was open for 0% of the time, Pallas kernels for 0%

commit v1 on v0

v1 whole, which is shorter than its diff:
```python
import functools

import jax
import jax.numpy as jnp
from jax import lax
from jax.experimental import pallas as pl
from jax.experimental.pallas import tpu as pltpu
from jax.sharding import PartitionSpec as P

MESH = pl.DeviceIdType.MESH
BF16 = jnp.bfloat16
F32 = jnp.float32
PARTS = 2
FT = 256
DC = 256
META = 16


def fit(total, wanted):
    return wanted if total % wanted == 0 else total


def kernel(
    dims,
    tok_in, meta_in, start_in, wg_hbm, wu_hbm, wd_hbm, out_ref,
    wg, wu, wd, tok, meta, xn, pos, wt, rows, hid, mmap, ycat,
    keep, px_out, px_in, y_out, y_in, z_out, z_in,
    w_sem, t_send, f_send, t_recv, m_send, m_recv,
    px_send, px_recv, y_send, y_recv, z_send, z_recv,
):
    chips, steps, cap, slots = dims
    local, width, ff = wg.shape
    toks = tok_in.shape[0]
    chunks = keep.shape[1]
    dc = keep.shape[3]
    ft = fit(ff, FT)
    part = toks // PARTS
    me = lax.axis_index("expert")
    now = lax.axis_index("tm")
    core = lax.rem(me, 2)
    chip = lax.div(me, 2)

    def peer(offset, other):
        own = (1 - core) if other else core
        return {"expert": lax.rem(chip + offset, chips) * 2 + own}

    def remote(src, dst, send, recv, where):
        return pltpu.make_async_remote_copy(
            src_ref=src, dst_ref=dst, send_sem=send, recv_sem=recv,
            device_id=where, device_id_type=MESH,
        )

    def weight_copy(kind, e):
        src, dst = ((wg_hbm, wg), (wu_hbm, wu), (wd_hbm, wd))[kind]
        return pltpu.make_async_copy(src.at[e], dst.at[e], w_sem.at[kind, e])

    for e in range(local):
        for kind in range(2):
            weight_copy(kind, e).start()
    for e in range(local):
        weight_copy(2, e).start()

    barrier = pltpu.get_barrier_semaphore()
    for d in range(chips):
        for other in (False, True):
            if d or other:
                pl.semaphore_signal(barrier, inc=1, device_id=peer(d, other), device_id_type=MESH)

    @pl.when(now > 0)
    def _():
        pl.semaphore_signal(barrier, inc=1, device_id={"tm": now - 1}, device_id_type=MESH)

    @pl.when(now < steps - 1)
    def _():
        pl.semaphore_signal(barrier, inc=1, device_id={"tm": now + 1}, device_id_type=MESH)

    peers = 2 * chips - 1 + jnp.where(now > 0, 1, 0) + jnp.where(now < steps - 1, 1, 0)
    pl.semaphore_wait(barrier, peers)

    def tok_copy(d, q):
        span = pl.ds(q * part, part)
        slot, side = ((chips - d) % chips, 0) if d else (0, 1)
        return remote(
            tok_in.at[span], tok.at[slot, side, span], t_send.at[d, q],
            t_recv.at[slot, side, q], peer(d, d == 0),
        )

    def meta_copy(d, other):
        slot, side = (chips - d) % chips, int(other)
        return remote(
            meta_in, meta.at[slot, side], m_send.at[d, side], m_recv.at[slot, side], peer(d, other)
        )

    def forward_copy(j, q):
        span = pl.ds(q * part, part)
        return remote(
            tok.at[j, 0, span], tok.at[j, 1, span], f_send.at[j, q], t_recv.at[j, 1, q],
            peer(0, True),
        )

    def tok_arrival(j, side, q):
        span = pl.ds(q * part, part)
        return remote(
            tok.at[j, side, span], tok.at[j, side, span], f_send.at[j, q],
            t_recv.at[j, side, q], peer(0, True),
        )

    def meta_arrival(j, side):
        return remote(
            meta_in, meta.at[j, side], m_send.at[0, 1], m_recv.at[j, side], peer(0, True)
        )

    meta_copy(0, True).start()
    for q in range(PARTS):
        tok_copy(0, q).start()
    for d in range(1, chips):
        for other in (False, True):
            meta_copy(d, other).start()
        for q in range(PARTS):
            tok_copy(d, q).start()

    def place(values, j, side):
        rows8 = pos.shape[2]
        names = (me * local + lax.broadcasted_iota(jnp.int32, (rows8, toks), 0)).astype(F32)
        member = jnp.zeros((rows8, toks), F32)
        weight = jnp.zeros((rows8, toks), F32)
        half = META // 2
        for k in range(half):
            hit = values[k : k + 1, :] == names
            member = member + jnp.where(hit, 1.0, 0.0)
            weight = weight + jnp.where(hit, values[half + k : half + k + 1, :], 0.0)
        earlier = (
            lax.broadcasted_iota(jnp.int32, (toks, toks), 0)
            < lax.broadcasted_iota(jnp.int32, (toks, toks), 1)
        )
        count = jnp.dot(
            member.astype(BF16), jnp.where(earlier, 1.0, 0.0).astype(BF16),
            preferred_element_type=F32,
        )
        pos[j, side] = jnp.where(member > 0.0, count, -4096.0)
        wt[j, side] = weight

    def normalise(src, j, side):
        group = 16

        def one(i, carry):
            span = pl.ds(pl.multiple_of(i * group, group), group)
            values = src[span, :].astype(F32)
            mean = jnp.mean(values * values, axis=-1, keepdims=True)
            into = pl.ds(pl.multiple_of(side * toks + i * group, group), group)
            xn[j, into, :] = (values * lax.rsqrt(mean + 1e-06)).astype(BF16)
            return carry

        lax.fori_loop(0, toks // group, one, 0)

    def gate_up(j, hs, first):
        rid = lax.broadcasted_iota(jnp.int32, (slots, toks), 0).astype(F32)

        def per_expert(e, carry):
            if first:
                for kind in range(2):
                    weight_copy(kind, e).wait()
            near = rid == pos[j, 0, pl.ds(e, 1), :]
            far = (rid - cap) == pos[j, 1, pl.ds(e, 1), :]
            chosen = jnp.concatenate(
                [jnp.where(near, 1.0, 0.0), jnp.where(far, 1.0, 0.0)], axis=1
            ).astype(BF16)
            scale = jnp.sum(
                jnp.where(near, wt[j, 0, pl.ds(e, 1), :], 0.0)
                + jnp.where(far, wt[j, 1, pl.ds(e, 1), :], 0.0),
                axis=1, keepdims=True,
            )
            mmap[hs, pl.ds(pl.multiple_of(e * slots, 16), slots), :] = chosen
            wide = fit(width, 512)

            def pick(i, c2):
                cols = pl.ds(pl.multiple_of(i * wide, 128), wide)
                rows[:, cols] = jnp.dot(
                    chosen, xn[j, :, cols], preferred_element_type=F32
                ).astype(BF16)
                return c2

            lax.fori_loop(0, width // wide, pick, 0)

            def tile(i, c2):
                cols = pl.ds(pl.multiple_of(i * ft, 128), ft)
                gate = jnp.dot(rows[...], wg[e, :, cols], preferred_element_type=F32)
                up = jnp.dot(rows[...], wu[e, :, cols], preferred_element_type=F32)
                hid[hs, e, :, cols] = (
                    gate / (1.0 + jnp.exp(-gate)) * up * scale
                ).astype(BF16)
                return c2

            lax.fori_loop(0, ff // ft, tile, 0)
            return carry

        lax.fori_loop(0, local, per_expert, 0)

    def pair_copy(j, k):
        return remote(
            px_out.at[j, k], px_in.at[j, k], px_send.at[j, k], px_recv.at[j, k], peer(0, True)
        )

    def back_copy(j, k):
        slot = chips - j
        return remote(
            y_out.at[j, k], y_in.at[slot, k], y_send.at[j, k], y_recv.at[slot, k], peer(j, False)
        )

    def rise_copy(k):
        return remote(
            z_out.at[k], z_in.at[k], z_send.at[k], z_recv.at[k], {"tm": lax.rem(now + 1, steps)}
        )

    def down(j, hs, k):
        cols = pl.ds(pl.multiple_of(k * dc, 128), dc)
        for e in range(local):
            ycat[e * slots : (e + 1) * slots, :] = jnp.dot(
                hid[hs, e], wd[e, :, cols], preferred_element_type=F32
            ).astype(BF16)
        share = lax.dot_general(
            mmap[hs], ycat[...], (((0,), (0,)), ((), ())), preferred_element_type=F32
        )
        px_out[j, k] = share[toks:].astype(BF16)
        keep[hs, k] = share[:toks]
        pair_copy(j, k).start()

    def send_back(j, k):
        pair_copy(j, k).wait_recv()
        y_out[j, k] = (keep[1, k] + px_in[j, k].astype(F32)).astype(BF16)
        back_copy(j, k).start()

    place(meta_in[...], 0, 0)
    normalise(tok_in, 0, 0)
    meta_arrival(0, 1).wait_recv()
    place(meta[0, 1], 0, 1)
    for q in range(PARTS):
        tok_arrival(0, 1, q).wait_recv()
    normalise(tok.at[0, 1], 0, 1)
    gate_up(0, 0, True)

    def far_chip(j, carry):
        for q in range(PARTS):
            tok_arrival(j, 0, q).wait_recv()
            forward_copy(j, q).start()
        for side in range(2):
            meta_arrival(j, side).wait_recv()
            place(meta[j, side], j, side)
        normalise(tok.at[j, 0], j, 0)
        for q in range(PARTS):
            tok_arrival(j, 1, q).wait_recv()
        normalise(tok.at[j, 1], j, 1)
        gate_up(j, 1, False)

        @pl.when(j == 1)
        def _():
            for e in range(local):
                weight_copy(2, e).wait()

        down(j, 1, 0)

        def step(k, c2):
            down(j, 1, k)
            send_back(j, k - 1)
            return c2

        lax.fori_loop(1, chunks, step, 0)
        send_back(j, chunks - 1)
        return carry

    lax.fori_loop(1, chips, far_chip, 0)

    if chips == 1:
        for e in range(local):
            weight_copy(2, e).wait()

    def own(k, carry):
        down(0, 0, k)
        return carry

    lax.fori_loop(0, chunks, own, 0)

    def finish(k, carry):
        cols = pl.ds(pl.multiple_of(k * dc, 128), dc)
        pair_copy(0, k).wait_recv()
        total = keep[0, k] + px_in[0, k].astype(F32)
        for j in range(1, chips):
            back_copy(chips - j, k).wait_recv()
            total = total + y_in[j, k].astype(F32)
        keep[0, k] = total

        @pl.when(now > 0)
        def _():
            rise_copy(k).wait_recv()
            keep[0, k] = keep[0, k] + z_in[k].astype(F32)

        @pl.when(now < steps - 1)
        def _():
            z_out[k] = keep[0, k].astype(BF16)
            rise_copy(k).start()

        out_ref[:, cols] = start_in[:, cols] + keep[0, k]
        return carry

    lax.fori_loop(0, chunks, finish, 0)

    meta_copy(0, True).wait_send()
    for q in range(PARTS):
        tok_copy(0, q).wait_send()
    for d in range(1, chips):
        for other in (False, True):
            meta_copy(d, other).wait_send()
        for q in range(PARTS):
            tok_copy(d, q).wait_send()
            forward_copy(d, q).wait_send()

    def drain(k, carry):
        for j in range(chips):
            pair_copy(j, k).wait_send()
            if j:
                back_copy(j, k).wait_send()

        @pl.when(now < steps - 1)
        def _():
            rise_copy(k).wait_send()

        return carry

    lax.fori_loop(0, chunks, drain, 0)


def shards(mesh, tokens, route_ids, route_probs, step_size, start_state, w_gate, w_up, w_down):
    toks, width = tokens.shape[1:]
    topk = route_ids.shape[2]
    local, _, ff = w_gate.shape
    group = mesh.shape["expert"]
    steps = mesh.shape["tm"]
    chips = group // 2
    cap = 3 * toks * topk // (2 * local * group)
    slots = -(-2 * cap // 16) * 16
    dc = fit(width, DC)
    chunks = width // dc
    half = META // 2
    local8 = -(-local // 8) * 8

    probs = route_probs[0]
    weights = step_size[0] * probs / jnp.sum(probs, axis=-1, keepdims=True)
    names = jnp.pad(route_ids[0].astype(F32), ((0, 0), (0, half - topk)), constant_values=-1.0)
    weights = jnp.pad(weights, ((0, 0), (0, half - topk)))
    meta = jnp.concatenate([names, weights], axis=1).T

    vmem = pl.BlockSpec(memory_space=pltpu.VMEM)
    hbm = pl.BlockSpec(memory_space=pl.ANY)
    dma = pltpu.SemaphoreType.DMA
    out = pl.pallas_call(
        functools.partial(kernel, (chips, steps, cap, slots)),
        out_shape=jax.ShapeDtypeStruct((toks, width), F32),
        in_specs=[vmem, vmem, vmem, hbm, hbm, hbm],
        out_specs=vmem,
        scratch_shapes=[
            pltpu.VMEM((local, width, ff), BF16),
            pltpu.VMEM((local, width, ff), BF16),
            pltpu.VMEM((local, ff, width), BF16),
            pltpu.VMEM((chips, 2, toks, width), BF16),
            pltpu.VMEM((chips, 2, META, toks), F32),
            pltpu.VMEM((chips, 2 * toks, width), BF16),
            pltpu.VMEM((chips, 2, local8, toks), F32),
            pltpu.VMEM((chips, 2, local8, toks), F32),
            pltpu.VMEM((slots, width), BF16),
            pltpu.VMEM((2, local, slots, ff), BF16),
            pltpu.VMEM((2, local * slots, 2 * toks), BF16),
            pltpu.VMEM((local * slots, dc), BF16),
            pltpu.VMEM((2, chunks, toks, dc), F32),
            pltpu.VMEM((chips, chunks, toks, dc), BF16),
            pltpu.VMEM((chips, chunks, toks, dc), BF16),
            pltpu.VMEM((chips, chunks, toks, dc), BF16),
            pltpu.VMEM((chips, chunks, toks, dc), BF16),
            pltpu.VMEM((chunks, toks, dc), BF16),
            pltpu.VMEM((chunks, toks, dc), BF16),
            dma((3, local)),
            dma((chips, PARTS)),
            dma((chips, PARTS)),
            dma((chips, 2, PARTS)),
            dma((chips, 2)),
            dma((chips, 2)),
            dma((chips, chunks)),
            dma((chips, chunks)),
            dma((chips, chunks)),
            dma((chips, chunks)),
            dma((chunks,)),
            dma((chunks,)),
        ],
        compiler_params=pltpu.CompilerParams(
            collective_id=0, has_side_effects=True, vmem_limit_bytes=67_043_328
        ),
    )(tokens[0], meta, start_state, w_gate, w_up, w_down)
    return out[None]


def solution(mesh):
    return jax.shard_map(
        functools.partial(shards, mesh),
        mesh=mesh,
        in_specs=(
            P("tm", ("copies", "expert"), None),
            P("tm", ("copies", "expert"), None),
            P("tm", ("copies", "expert"), None),
            P(("copies", "tm")),
            P(("copies", "expert"), None),
            P("expert", None, None),
            P("expert", None, None),
            P("expert", None, None),
        ),
        out_specs=P("tm", ("copies", "expert"), None),
        check_vma=False,
    )
```

time: 237 us -> 68 us (0.29); the launches traced: 233 us -> 67.7 us
  waiting for transfers between devices: 96.5 us -> 0 us
  Pallas kernels: 0 us -> 62.1 us
  blocking collectives: 56.6 us -> 0 us
  matrix products: 29.9 us -> 0 us
  local copies, waits for them, and re-layouts: 22.6 us -> 2.3 us
  between operations: 14.2 us -> 0.66 us
  other arithmetic: 8.19 us -> 2.69 us
  starting transfers between devices: 5.28 us -> 0 us
    pallas_call x0 -> x1, Pallas kernels: none -> 62.1 us  [shards(): pl.pallas_call(functools.partial(kernel, (chips, steps, cap, slots)), out...]
    all_to_all x1 -> x0, blocking collectives: 56.6 us -> none  [shards(): lax.all_to_all(outgoing, 'expert', split_axis=0, concat_axis=1, tiled=True)]
    all_to_all x1 -> x0, waiting for transfers between devices: 52.6 us -> none  [shards(): lax.all_to_all(answered, 'expert', split_axis=1, concat_axis=0, tiled=True)]
    all_gather x1 -> x0, waiting for transfers between devices: 43.9 us -> none  [shards(): lax.all_gather(increment[None].astype(jnp.bfloat16), 'tm', axis=0, tiled=...]
    dot_general x4 -> x0, matrix products: 29.9 us -> none  [the longest x1 15.9 us: expert_rows(): jnp.einsum('jrf,jfd->jrd', hidden, w_down, preferred_element_type=jnp.flo...]
    gather x1 -> x0, local copies, waits for them, and re-layouts: 9.28 us -> none  [shards(): returned.reshape(expert_total * capacity, feature_count)[slot_index]]
    reshape x2 -> x0, local copies, waits for them, and re-layouts: 8.09 us -> none  [the longest x1 5.23 us: expert_rows(): result.astype(jnp.bfloat16)]
    all_to_all x1 -> x0, starting transfers between devices: 5.06 us -> none  [shards(): lax.all_to_all(answered, 'expert', split_axis=1, concat_axis=0, tiled=True)]
  transfers between devices with their start and end apart: 2 -> 0, of which waited for: 2 -> 0; matrix products, arithmetic and copies ran while one was open for 0% -> 0% of each run, Pallas kernels for 0% -> 0%
where the time goes in v1:
time: 68 us; the launch traced here: 67.7 us
  Pallas kernels  62.1 us (91%)
  other arithmetic  2.69 us (4%)
  local copies, waits for them, and re-layouts  2.3 us (3%)
    pallas_call x1, Pallas kernels, shards(): pl.pallas_call(functools.partial(kernel, (chips, steps, cap, slots)), out...  62.1 us
    unnamed x1, local copies, waits for them, and re-layouts  2.3 us

profile of v1, /device:TPU:24, one launch (start us, length us, event | category | flops | bytes accessed | tf_op | source)
XLA Modules:
  0.0 67.7 jit_solution(856108914209314327)
XLA Ops:
  0.7 0.7 %reduce_sum.9 = f32[128]{0:T(128)S(1)} reduce(f32[1,128,6]{1,0,2:T(1,128)} %param.10, f32[]{:T(128)} %constant.1.clone.1), dimensions={0,2}, to_apply=%region_0.0 | reduce | flops 640 | bytes 3588 | tf_op jit(solution)/shard_map/reduce_sum | solution.py:347
  1.4 0.7 %bitcast_divide_fusion = f32[128,6]{0,1:T(8,128)S(1)} fusion(f32[1,128,6]{1,0,2:T(1,128)} %param.10, f32[128]{0:T(128)S(1)} %reduce_sum.9, f32[]{:T(128)} %bitcast.9), kind=kLoop, calls=%fused_computation.4 | loop fusion | flops 1536 | bytes 6660 | tf_op jit(solution)/shard_map/div | solution.py:347
  2.0 0.7 %fusion.1 = f32[128,6]{0,1:T(8,128)S(1)} fusion(s32[1,128,6]{1,0,2:T(1,128)} %param.9), kind=kLoop, calls=%fused_computation.7 | loop fusion | flops 768 | bytes 6144 | tf_op jit(solution)/shard_map/convert_element_type | solution.py:348
  2.7 0.6 fusion.meta_in
  3.3 62.1 %shard_map.82 = f32[128,2048]{1,0:T(8,128)} custom-call(bf16[128,2048]{1,0:T(8,128)(2,1)} %bitcast.11, f32[16,128]{1,0:T(8,128)} %fusion.meta_in, f32[128,2048]{1,0:T(8,128)} %start_in.1, bf16[4,2048,768]{2,1,0:T(8,128)(2,1)} %wg_hbm.1, bf16[4,2048,768]{2,1,0:T(8,128)(2,1)} %wu_hbm.1, bf16[4,768,2048]{2,1,0:T(8,128)(2,1)} %wd_hbm.1), custom_call_target="tpu_custom_call" | custom-call | tf_op jit(solution)/shard_map/pallas_call | solution.py:355
  65.4 2.3 %copy.19 = f32[1,128,2048]{2,1,0:T(8,128)} copy(f32[1,128,2048]{2,1,0:T(8,128)} %bitcast.10) | data formatting | bytes 2097152

commit v2 on v1

v2 whole, which is shorter than its diff:
```python
import functools

import jax
import jax.numpy as jnp
from jax import lax
from jax.experimental import pallas as pl
from jax.experimental.pallas import tpu as pltpu
from jax.sharding import PartitionSpec as P

MESH = pl.DeviceIdType.MESH
BF16 = jnp.bfloat16
F32 = jnp.float32
COLS = 512
FT = 384
DC = 256


def fit(total, wanted):
    return wanted if total % wanted == 0 else total


def kernel(
    dims,
    tok_in, ids_in, probs_in, step_in, wg_hbm, wu_hbm, wd_hbm, out_ref,
    wg, wu, wd, tok, ids, probs, scale, squares, rows, acc_g, acc_u, hid, mmap, ycat,
    keep, px_out, px_in, y_out, y_in, z_out, z_in,
    up_sem, down_sem, t_send, f_send, t_recv, i_send, i_recv, p_send, p_recv,
    px_send, px_recv, y_send, y_recv, z_send, z_recv,
):
    chips, steps, cap, slots = dims
    local, width, ff = wg.shape
    toks = tok_in.shape[0]
    topk = ids_in.shape[0]
    parts, cq = tok.shape[1], tok.shape[3]
    chunks, dc = keep.shape[1], keep.shape[3]
    ft = fit(ff, FT)
    me = lax.axis_index("expert")
    now = lax.axis_index("tm")
    core = lax.rem(me, 2)
    chip = lax.div(me, 2)

    def peer(offset, other):
        own = (1 - core) if other else core
        return {"expert": lax.rem(chip + offset, chips) * 2 + own}

    def remote(src, dst, send, recv, where):
        return pltpu.make_async_remote_copy(
            src_ref=src, dst_ref=dst, send_sem=send, recv_sem=recv,
            device_id=where, device_id_type=MESH,
        )

    def up_copy(kind, e, q):
        src, dst = ((wg_hbm, wg), (wu_hbm, wu))[kind]
        span = pl.ds(pl.multiple_of(q * cq, 128), cq)
        return pltpu.make_async_copy(src.at[e, span], dst.at[e, span], up_sem.at[kind, e, q])

    def down_copy(e):
        return pltpu.make_async_copy(wd_hbm.at[e], wd.at[e], down_sem.at[e])

    for q in range(parts):
        for e in range(local):
            for kind in range(2):
                up_copy(kind, e, q).start()
    for e in range(local):
        down_copy(e).start()

    barrier = pltpu.get_barrier_semaphore()
    for d in range(chips):
        for other in (False, True):
            if d or other:
                pl.semaphore_signal(barrier, inc=1, device_id=peer(d, other), device_id_type=MESH)

    @pl.when(now > 0)
    def _():
        pl.semaphore_signal(barrier, inc=1, device_id={"tm": now - 1}, device_id_type=MESH)

    @pl.when(now < steps - 1)
    def _():
        pl.semaphore_signal(barrier, inc=1, device_id={"tm": now + 1}, device_id_type=MESH)

    peers = 2 * chips - 1 + jnp.where(now > 0, 1, 0) + jnp.where(now < steps - 1, 1, 0)
    pl.semaphore_wait(barrier, peers)

    def tok_copy(d, q):
        slot, side = ((chips - d) % chips, 0) if d else (0, 1)
        return remote(
            tok_in.at[:, pl.ds(q * cq, cq)], tok.at[slot, q, pl.ds(side * toks, toks)],
            t_send.at[d, q], t_recv.at[slot, side, q], peer(d, d == 0),
        )

    def route_copies(d, other):
        slot, side = (chips - d) % chips, int(other)
        where = peer(d, other)
        return (
            remote(ids_in, ids.at[slot, side], i_send.at[d, side], i_recv.at[slot, side], where),
            remote(
                probs_in, probs.at[slot, side], p_send.at[d, side], p_recv.at[slot, side], where
            ),
        )

    def forward_copy(j, q):
        return remote(
            tok.at[j, q, pl.ds(0, toks)], tok.at[j, q, pl.ds(toks, toks)],
            f_send.at[j, q], t_recv.at[j, 1, q], peer(0, True),
        )

    def tok_arrival(j, side, q):
        span = tok.at[j, q, pl.ds(side * toks, toks)]
        return remote(span, span, f_send.at[j, q], t_recv.at[j, side, q], peer(0, True))

    def route_arrivals(j, side):
        where = peer(0, True)
        return (
            remote(ids_in, ids.at[j, side], i_send.at[0, 1], i_recv.at[j, side], where),
            remote(probs_in, probs.at[j, side], p_send.at[0, 1], p_recv.at[j, side], where),
        )

    for d in range(chips):
        for other in (False, True):
            if d or other:
                for copy in route_copies(d, other):
                    copy.start()
    for q in range(parts):
        for d in range(1, chips):
            tok_copy(d, q).start()
        tok_copy(0, q).start()

    for q in range(parts):
        tok[0, q, pl.ds(0, toks), :] = tok_in[:, q * cq : (q + 1) * cq]

    local8 = scale.shape[0]
    earlier = jnp.where(
        lax.broadcasted_iota(jnp.int32, (toks, toks), 0)
        < lax.broadcasted_iota(jnp.int32, (toks, toks), 1),
        1.0, 0.0,
    ).astype(BF16)
    rid = lax.broadcasted_iota(jnp.int32, (slots, toks), 0).astype(F32)
    names = me * local + lax.broadcasted_iota(jnp.int32, (local8, toks), 0)
    step_now = step_in[0]

    def place(id_ref, prob_ref):
        member = jnp.zeros((local8, toks), F32)
        weight = jnp.zeros((local8, toks), F32)
        total = jnp.zeros((1, toks), F32)
        for k in range(topk):
            hit = id_ref[k] == names
            member = member + jnp.where(hit, 1.0, 0.0)
            weight = weight + jnp.where(hit, prob_ref[k], 0.0)
            total = total + prob_ref[k]
        count = jnp.dot(member.astype(BF16), earlier, preferred_element_type=F32)
        return jnp.where(member > 0.0, count, -4096.0), weight * (step_now / total)

    def tables(j, near, far):
        for e in range(local):
            low = rid == near[0][e : e + 1, :]
            high = (rid - cap) == far[0][e : e + 1, :]
            mmap[j, e * slots : (e + 1) * slots, :] = jnp.concatenate(
                [jnp.where(low, 1.0, 0.0), jnp.where(high, 1.0, 0.0)], axis=1
            ).astype(BF16)
            amount = jnp.sum(
                jnp.where(low, near[1][e : e + 1, :], 0.0)
                + jnp.where(high, far[1][e : e + 1, :], 0.0),
                axis=1, keepdims=True,
            )
            scale[e, pl.ds(pl.multiple_of(j * slots, 16), slots), :] = jnp.broadcast_to(
                amount, (slots, 128)
            )

    mine = place(ids_in, probs_in)
    for copy in route_arrivals(0, 1):
        copy.wait_recv()
    tables(0, mine, place(ids.at[0, 1], probs.at[0, 1]))

    def clear(e, carry):
        acc_g[e] = jnp.zeros(acc_g.shape[1:], F32)
        acc_u[e] = jnp.zeros(acc_u.shape[1:], F32)
        squares[e] = jnp.zeros(squares.shape[1:], F32)
        return carry

    lax.fori_loop(0, local, clear, 0)

    def far_tables(j, carry):
        for side in range(2):
            for copy in route_arrivals(j, side):
                copy.wait_recv()
        tables(j, place(ids.at[j, 0], probs.at[j, 0]), place(ids.at[j, 1], probs.at[j, 1]))
        return carry

    lax.fori_loop(1, chips, far_tables, 0)

    def pass_on(q):
        for j in range(1, chips):
            tok_arrival(j, 0, q).wait_recv()
            forward_copy(j, q).start()

    pass_on(0)

    def gather_step(q, carry):
        tok_arrival(0, 1, q).wait_recv()
        for j in range(1, chips):
            tok_arrival(j, 1, q).wait_recv()
        span = pl.ds(pl.multiple_of(q * cq, 128), cq)

        def per_expert(e, c2):
            for kind in range(2):
                up_copy(kind, e, q).wait()
            for j in range(chips):
                chosen = mmap[j, pl.ds(pl.multiple_of(e * slots, 16), slots), :]
                rows[j * slots : (j + 1) * slots, :] = jnp.dot(
                    chosen, tok[j, q], preferred_element_type=F32
                ).astype(BF16)
            sums = squares[e]
            for i in range(cq // 128):
                piece = rows[:, i * 128 : (i + 1) * 128].astype(F32)
                sums = sums + piece * piece
            squares[e] = sums
            for i in range(ff // ft):
                cols = pl.ds(i * ft, ft)
                acc_g[e, :, cols] += jnp.dot(
                    rows[...], wg[e, span, cols], preferred_element_type=F32
                )
                acc_u[e, :, cols] += jnp.dot(
                    rows[...], wu[e, span, cols], preferred_element_type=F32
                )

            @pl.when((e == local // 2) & (q < parts - 1))
            def _():
                pass_on(q + 1)

            return c2

        lax.fori_loop(0, local, per_expert, 0)
        return carry

    lax.fori_loop(0, parts, gather_step, 0)

    def activate(e, carry):
        mean = jnp.sum(squares[e], axis=1, keepdims=True) * (1.0 / width)
        root = lax.rsqrt(mean + 1e-06)
        amount = root * scale[e, :, 0:1]
        for i in range(ff // 128):
            cols = pl.ds(i * 128, 128)
            gate = acc_g[e, :, cols] * root
            hid[e, :, cols] = (
                gate / (1.0 + jnp.exp(-gate)) * (acc_u[e, :, cols] * amount)
            ).astype(BF16)
        return carry

    lax.fori_loop(0, local, activate, 0)

    for e in range(local):
        down_copy(e).wait()

    def pair_copy(j, k):
        return remote(
            px_out.at[j, k], px_in.at[j, k], px_send.at[j, k], px_recv.at[j, k], peer(0, True)
        )

    def back_copy(j, k):
        slot = chips - j
        return remote(
            y_out.at[j, k], y_in.at[slot, k], y_send.at[j, k], y_recv.at[slot, k], peer(j, False)
        )

    def rise_copy(k):
        return remote(
            z_out.at[k], z_in.at[k], z_send.at[k], z_recv.at[k], {"tm": lax.rem(now + 1, steps)}
        )

    def down(k):
        cols = pl.ds(pl.multiple_of(k * dc, 128), dc)
        for e in range(local):
            result = jnp.dot(hid[e], wd[e, :, cols], preferred_element_type=F32).astype(BF16)
            for j in range(chips):
                ycat[j, e * slots : (e + 1) * slots, :] = result[j * slots : (j + 1) * slots]
        for j in [*range(1, chips), 0]:
            share = lax.dot_general(
                mmap[j], ycat[j], (((0,), (0,)), ((), ())), preferred_element_type=F32
            )
            px_out[j, k] = share[toks:].astype(BF16)
            keep[j, k] = share[:toks]
            pair_copy(j, k).start()

    def send_back(k):
        for j in range(1, chips):
            pair_copy(j, k).wait_recv()
            y_out[j, k] = (keep[j, k] + px_in[j, k].astype(F32)).astype(BF16)
            back_copy(j, k).start()

    down(0)

    def step(k, carry):
        down(k)
        send_back(k - 1)
        return carry

    lax.fori_loop(1, chunks, step, 0)
    send_back(chunks - 1)

    def finish(k, carry):
        cols = pl.ds(pl.multiple_of(k * dc, 128), dc)
        pair_copy(0, k).wait_recv()
        total = keep[0, k] + px_in[0, k].astype(F32)
        for j in range(1, chips):
            back_copy(chips - j, k).wait_recv()
            total = total + y_in[j, k].astype(F32)
        keep[0, k] = total

        @pl.when(now > 0)
        def _():
            rise_copy(k).wait_recv()
            keep[0, k] = keep[0, k] + z_in[k].astype(F32)

        @pl.when(now < steps - 1)
        def _():
            z_out[k] = keep[0, k].astype(BF16)
            rise_copy(k).start()

        out_ref[:, cols] = keep[0, k]
        return carry

    lax.fori_loop(0, chunks, finish, 0)

    for d in range(chips):
        for other in (False, True):
            if d or other:
                for copy in route_copies(d, other):
                    copy.wait_send()
        for q in range(parts):
            tok_copy(d, q).wait_send()
            if d:
                forward_copy(d, q).wait_send()

    def drain(k, carry):
        for j in range(chips):
            pair_copy(j, k).wait_send()
            if j:
                back_copy(j, k).wait_send()

        @pl.when(now < steps - 1)
        def _():
            rise_copy(k).wait_send()

        return carry

    lax.fori_loop(0, chunks, drain, 0)


def shards(mesh, tokens, route_ids, route_probs, step_size, start_state, w_gate, w_up, w_down):
    toks, width = tokens.shape[1:]
    topk = route_ids.shape[2]
    local, _, ff = w_gate.shape
    group = mesh.shape["expert"]
    steps = mesh.shape["tm"]
    chips = group // 2
    cap = 3 * toks * topk // (2 * local * group)
    slots = -(-2 * cap // 16) * 16
    dc, cq = fit(width, DC), fit(width, COLS)
    chunks, parts = width // dc, width // cq
    local8 = -(-local // 8) * 8

    vmem = pl.BlockSpec(memory_space=pltpu.VMEM)
    smem = pl.BlockSpec(memory_space=pltpu.SMEM)
    hbm = pl.BlockSpec(memory_space=pl.ANY)
    dma = pltpu.SemaphoreType.DMA
    total = pl.pallas_call(
        functools.partial(kernel, (chips, steps, cap, slots)),
        out_shape=jax.ShapeDtypeStruct((toks, width), F32),
        in_specs=[vmem, vmem, vmem, smem, hbm, hbm, hbm],
        out_specs=vmem,
        scratch_shapes=[
            pltpu.VMEM((local, width, ff), BF16),
            pltpu.VMEM((local, width, ff), BF16),
            pltpu.VMEM((local, ff, width), BF16),
            pltpu.VMEM((chips, parts, 2 * toks, cq), BF16),
            pltpu.VMEM((chips, 2, topk, 1, toks), jnp.int32),
            pltpu.VMEM((chips, 2, topk, 1, toks), F32),
            pltpu.VMEM((local8, chips * slots, 128), F32),
            pltpu.VMEM((local, chips * slots, 128), F32),
            pltpu.VMEM((chips * slots, cq), BF16),
            pltpu.VMEM((local, chips * slots, ff), F32),
            pltpu.VMEM((local, chips * slots, ff), F32),
            pltpu.VMEM((local, chips * slots, ff), BF16),
            pltpu.VMEM((chips, local * slots, 2 * toks), BF16),
            pltpu.VMEM((chips, local * slots, dc), BF16),
            pltpu.VMEM((chips, chunks, toks, dc), F32),
            pltpu.VMEM((chips, chunks, toks, dc), BF16),
            pltpu.VMEM((chips, chunks, toks, dc), BF16),
            pltpu.VMEM((chips, chunks, toks, dc), BF16),
            pltpu.VMEM((chips, chunks, toks, dc), BF16),
            pltpu.VMEM((chunks, toks, dc), BF16),
            pltpu.VMEM((chunks, toks, dc), BF16),
            dma((2, local, parts)),
            dma((local,)),
            dma((chips, parts)),
            dma((chips, parts)),
            dma((chips, 2, parts)),
            dma((chips, 2)),
            dma((chips, 2)),
            dma((chips, 2)),
            dma((chips, 2)),
            dma((chips, chunks)),
            dma((chips, chunks)),
            dma((chips, chunks)),
            dma((chips, chunks)),
            dma((chunks,)),
            dma((chunks,)),
        ],
        compiler_params=pltpu.CompilerParams(
            collective_id=0, has_side_effects=True, vmem_limit_bytes=67_043_328
        ),
    )(
        tokens[0], jnp.transpose(route_ids, (2, 0, 1)), jnp.transpose(route_probs, (2, 0, 1)),
        step_size, w_gate, w_up, w_down,
    )
    return (start_state + total)[None]


def solution(mesh):
    return jax.shard_map(
        functools.partial(shards, mesh),
        mesh=mesh,
        in_specs=(
            P("tm", ("copies", "expert"), None),
            P("tm", ("copies", "expert"), None),
            P("tm", ("copies", "expert"), None),
            P(("copies", "tm")),
            P(("copies", "expert"), None),
            P("expert", None, None),
            P("expert", None, None),
            P("expert", None, None),
        ),
        out_specs=P("tm", ("copies", "expert"), None),
        check_vma=False,
    )
```

time: 68 us -> 63.4 us (0.932)
  local copies, waits for them, and re-layouts: 2.3 us -> 0 us
  Pallas kernels: 62.1 us -> 59.9 us
    broadcast_in_dim x0 -> x1, other arithmetic: none -> 2.64 us  [shards(): return (start_state + total)[None]]
    unnamed x1 -> x0, local copies, waits for them, and re-layouts: 2.3 us -> none
    pallas_call x1, Pallas kernels: 62.1 us -> 59.9 us  [shards(): pl.pallas_call(functools.partial(kernel, (chips, steps, cap, slots)), out...]
    reduce_sum x1 -> x0, other arithmetic: 0.71 us -> none  [shards(): weights = step_size[0] * probs / jnp.sum(probs, axis=-1, keepdims=True)]
    convert_element_type x1 -> x0, other arithmetic: 0.69 us -> none  [shards(): route_ids[0].astype(F32)]
    div x1 -> x0, other arithmetic: 0.69 us -> none  [shards(): weights = step_size[0] * probs / jnp.sum(probs, axis=-1, keepdims=True)]
where the time goes in v2:
time: 63.4 us; the launch traced here: 63.3 us
  Pallas kernels  59.9 us (94%)
  other arithmetic  2.64 us (4%)
  between operations  0.66 us (1%)
    pallas_call x1, Pallas kernels, shards(): pl.pallas_call(functools.partial(kernel, (chips, steps, cap, slots)), out...  59.9 us
    broadcast_in_dim x1, other arithmetic, shards(): return (start_state + total)[None]  2.64 us

profile of v2, /device:TPU:24, one launch (start us, length us, event | category | flops | bytes accessed | tf_op | source)
XLA Modules:
  0.0 63.3 jit_solution(3307955964103116055)
XLA Ops:
  0.7 59.9 %shard_map.82 = f32[128,2048]{1,0:T(8,128)} custom-call(bf16[128,2048]{1,0:T(8,128)(2,1)} %bitcast.5, s32[6,1,128]{2,1,0:T(1,128)} %bitcast.6, f32[6,1,128]{2,1,0:T(1,128)} %bitcast.7, f32[1]{0:T(128)S(6)} %copy.9.step_in, bf16[4,2048,768]{2,1,0:T(8,128)(2,1)} %wg_hbm.1, bf16[4,2048,768]{2,1,0:T(8,128)(2,1)} %wu_hbm.1, bf16[4,768,2048]{2,1,0:T(8,128)(2,1)} %wd_hbm.1), custom_call_target="tpu_custom_call" | custom-call | tf_op jit(solution)/shard_map/pallas_call | solution.py:366
  60.6 2.6 %add_bitcast_fusion = f32[1,128,2048]{2,1,0:T(8,128)} fusion(f32[128,2048]{1,0:T(8,128)} %param.12, f32[128,2048]{1,0:T(8,128)} %shard_map.82), kind=kLoop, calls=%fused_computation | loop fusion | flops 262144 | bytes 3145728 | tf_op jit(solution)/shard_map/broadcast_in_dim | solution.py:416

commit v3 on v2

--- a/solution.py
+++ b/solution.py
@@ -11,7 +11,7 @@
 BF16 = jnp.bfloat16
 F32 = jnp.float32
 COLS = 512
-FT = 384
+FT = 768
 DC = 256
 
 

time: 63.4 us -> 61 us (0.962)
  Pallas kernels: 59.9 us -> 57.5 us
    pallas_call x1, Pallas kernels: 59.9 us -> 57.5 us  [shards(): pl.pallas_call(functools.partial(kernel, (chips, steps, cap, slots)), out...]
where the time goes in v3:
time: 61 us; the launch traced here: 60.8 us
  Pallas kernels  57.5 us (94%)
  other arithmetic  2.64 us (4%)
  between operations  0.66 us (1%)
    pallas_call x1, Pallas kernels, shards(): pl.pallas_call(functools.partial(kernel, (chips, steps, cap, slots)), out...  57.5 us
    broadcast_in_dim x1, other arithmetic, shards(): return (start_state + total)[None]  2.64 us

profile of v3, /device:TPU:24, one launch (start us, length us, event | category | flops | bytes accessed | tf_op | source)
XLA Modules:
  0.0 60.8 jit_solution(16810954957809402927)
XLA Ops:
  0.7 57.5 %shard_map.82 = f32[128,2048]{1,0:T(8,128)} custom-call(bf16[128,2048]{1,0:T(8,128)(2,1)} %bitcast.5, s32[6,1,128]{2,1,0:T(1,128)} %bitcast.6, f32[6,1,128]{2,1,0:T(1,128)} %bitcast.7, f32[1]{0:T(128)S(6)} %copy.9.step_in, bf16[4,2048,768]{2,1,0:T(8,128)(2,1)} %wg_hbm.1, bf16[4,2048,768]{2,1,0:T(8,128)(2,1)} %wu_hbm.1, bf16[4,768,2048]{2,1,0:T(8,128)(2,1)} %wd_hbm.1), custom_call_target="tpu_custom_call" | custom-call | tf_op jit(solution)/shard_map/pallas_call | solution.py:366
  58.1 2.6 %add_bitcast_fusion = f32[1,128,2048]{2,1,0:T(8,128)} fusion(f32[128,2048]{1,0:T(8,128)} %param.12, f32[128,2048]{1,0:T(8,128)} %shard_map.82), kind=kLoop, calls=%fused_computation | loop fusion | flops 262144 | bytes 3145728 | tf_op jit(solution)/shard_map/broadcast_in_dim | solution.py:416
